TPU v7x, 256 devices: a whole 4x4x8 slice. The times are simulated.
256 devices in a mesh: wide: 64 (over y, z, core), narrow: 4 (over x).
Axes of the slice: x: 4, y: 4, z: 8, core: 2. Of those that a mesh axis runs over, the one named last changes fastest.
Arguments:
- residual_in: bfloat16 [128, 7168], P('wide', 'narrow'), may hold values from -2 to 2
- query_nope: bfloat16 [128, 64, 128], P('wide', 'narrow'), may hold values from -6 to 6
- query_rope: bfloat16 [128, 64, 64], P('wide', 'narrow'), may hold values from -8 to 8
- absorb_key: bfloat16 [64, 128, 512], P('narrow'), may hold values from -0.5 to 0.5
- absorb_value: bfloat16 [64, 512, 128], P('narrow'), may hold values from -0.25 to 0.25
- latent_cache: bfloat16 [128, 2048, 576], P('wide'), may hold values from -8 to 8
- cache_lengths: int32 [128], P('wide'), may hold values from 256 to 2048, as said below
- slot_rows: int32 [128], replicated, may hold values from 0 to 127, each once
- out_proj: bfloat16 [8192, 7168], P('wide', 'narrow'), may hold values from -0.0625 to 0.0625
- norm_gain: bfloat16 [7168], P('narrow'), may hold values from 0.25 to 1.75
- gate_weight: bfloat16 [7168, 18432], P('narrow', 'wide'), may hold values from -0.0625 to 0.0625
- up_weight: bfloat16 [7168, 18432], P('narrow', 'wide'), may hold values from -0.0625 to 0.0625
- down_weight: bfloat16 [18432, 7168], P('wide', 'narrow'), may hold values from -0.046875 to 0.046875
Outputs:
- residual_out: bfloat16 [128, 7168], P('wide', 'narrow')
Inputs may be any that keep to these rules, and one draw needn't show every extreme that they name: `cache_lengths`: every slot has at least 256 live positions; in every draw some slot is full. `slot_rows`: each batch row is named by exactly one slot.
All inputs are finite; a program needn't handle non-finite values.
Results may differ from a plain program's by a relative error of at most 0.009.
Values may be sent and summed in bfloat16 or wider, within the bound.
A program may use at most 64 MiB of HBM per device.

v0:
```python
import math
import jax
import jax.numpy as jnp
from jax import lax
from jax.sharding import PartitionSpec as P

D = 7168


def shards(
    residual_in,
    query_nope,
    query_rope,
    absorb_key,
    absorb_value,
    latent_cache,
    cache_lengths,
    slot_rows,
    out_proj,
    norm_gain,
    gate_weight,
    up_weight,
    down_weight,
):
    slot_count = latent_cache.shape[0]
    head_size = query_nope.shape[2]
    latent_width = absorb_key.shape[2]
    group_index = lax.axis_index("wide")
    packed_queries = jnp.concatenate([query_nope, query_rope], axis=2)
    gathered = lax.all_gather(packed_queries, "wide", axis=0, tiled=True)
    my_rows = lax.dynamic_slice_in_dim(slot_rows, group_index * slot_count, slot_count)
    selected = jnp.take(gathered, my_rows, axis=0)
    query_latent = jnp.einsum(
        "rhd,hdc->rhc", selected[:, :, :head_size], absorb_key, preferred_element_type=jnp.float32
    ).astype(jnp.bfloat16)
    full_query = jnp.concatenate([query_latent, selected[:, :, head_size:]], axis=2)
    scale = 1.0 / math.sqrt(full_query.shape[2] - latent_width + head_size)
    scores = (
        jnp.einsum("rhc,rtc->rht", full_query, latent_cache, preferred_element_type=jnp.float32)
        * scale
    )
    positions = jnp.arange(latent_cache.shape[1], dtype=jnp.int32)
    live = positions[None, None, :] < cache_lengths[:, None, None]
    scores = jnp.where(live, scores, -jnp.inf)
    highest = jnp.max(scores, axis=2, keepdims=True)
    weights = jnp.where(live, jnp.exp(scores - highest), 0.0)
    probs = (weights / jnp.sum(weights, axis=2, keepdims=True)).astype(jnp.bfloat16)
    context = jnp.einsum("rht,rtc->rhc", probs, latent_cache, preferred_element_type=jnp.float32)
    context = context[:, :, :latent_width].astype(jnp.bfloat16)
    heads_out = jnp.einsum(
        "rhc,hcd->rhd", context, absorb_value, preferred_element_type=jnp.float32
    ).astype(jnp.bfloat16)
    every_head = lax.all_gather(heads_out, "narrow", axis=1, tiled=True)
    flat_heads = every_head.reshape(slot_count, -1)
    head_columns = lax.all_to_all(flat_heads, "wide", split_axis=1, concat_axis=0, tiled=True)
    inverse = jnp.argsort(slot_rows)
    attention = lax.psum_scatter(
        jnp.dot(
            jnp.take(head_columns, inverse, axis=0), out_proj, preferred_element_type=jnp.float32
        ),
        "wide",
        scatter_dimension=0,
        tiled=True,
    )
    middle = residual_in.astype(jnp.float32) + attention
    square_sum = lax.psum(jnp.sum(middle * middle, axis=1), "narrow")
    normed = (
        middle * lax.rsqrt(square_sum / D + 1e-06)[:, None] * norm_gain.astype(jnp.float32)
    ).astype(jnp.bfloat16)
    hidden_cols = gate_weight.shape[1]
    row_piece = lax.all_gather(normed, "wide", axis=0, tiled=True)
    local_terms = jnp.concatenate(
        [
            jnp.dot(row_piece, gate_weight, preferred_element_type=jnp.float32),
            jnp.dot(row_piece, up_weight, preferred_element_type=jnp.float32),
        ],
        axis=1,
    )
    summed = lax.psum(local_terms, "narrow")
    hidden = (jax.nn.silu(summed[:, :hidden_cols]) * summed[:, hidden_cols:]).astype(jnp.bfloat16)
    ffn_total = lax.psum_scatter(
        jnp.dot(hidden, down_weight, preferred_element_type=jnp.float32),
        "wide",
        scatter_dimension=0,
        tiled=True,
    )
    return (middle + ffn_total).astype(jnp.bfloat16)


def solution(mesh):
    in_specs = (
        P("wide", "narrow"),
        P("wide", "narrow", None),
        P("wide", "narrow", None),
        P("narrow", None, None),
        P("narrow", None, None),
        P("wide", None, None),
        P("wide"),
        P(),
        P("wide", "narrow"),
        P("narrow"),
        P("narrow", "wide"),
        P("narrow", "wide"),
        P("wide", "narrow"),
    )
    out_specs = P("wide", "narrow")
    return jax.shard_map(shards, mesh=mesh, in_specs=in_specs, out_specs=out_specs, check_vma=False)
```

profile of v0, /device:TPU:2, one launch (start us, length us, event | category | flops | bytes accessed | tf_op | source)
XLA Modules:
  0.0 592.2 jit_solution(973563443931683544)
XLA Ops:
  6.5 0.9 compare_and_fusion
  7.4 0.7 pad_maximum_fusion.1
  8.2 53.8 %all_gather.9 = bf16[128,16,192]{2,1,0:T(8,128)(2,1)S(1)} all-gather(bf16[2,16,192]{2,1,0:T(8,128)(2,1)S(1)} %pad_maximum_fusion.1), channel_id=1, replica_groups=mesh['wide'=64,'narrow'=4] {'wide'}, dimensions={0}, use_global_device_ids=true | all-gather | bytes 798720 | tf_op jit(solution)/shard_map/all_gather | solution.py:30
  62.6 0.7 iota_compare_fusion
  63.7 3.1 fusion.4
  67.0 3.7 fusion.7
  70.8 2.0 fusion.5
  72.8 12.7 %all_gather.10 = bf16[2,64,128]{2,0,1:T(2,128)(2,1)} all-gather(bf16[2,16,128]{2,0,1:T(2,128)(2,1)S(1)} %fusion.5), channel_id=1, replica_groups=mesh['wide'=64,'narrow'=4] {'narrow'}, dimensions={1}, use_global_device_ids=true | all-gather | bytes 40960 | tf_op jit(solution)/shard_map/all_gather | solution.py:53
  85.6 6.7 %all-to-all-start = ((bf16[2,64,128]{2,0,1:T(2,128)(2,1)}), bf16[2,64,128]{2,0,1:T(2,128)(2,1)S(1)}, u32[]{:S(2)}, u32[]{:S(2)}) async-start(bf16[2,64,128]{2,0,1:T(2,128)(2,1)} %all_gather.10), calls=%async_computation | async-start | bytes 65536 | tf_op jit(solution)/shard_map/all_to_all | solution.py:55
  92.4 2.5 sort.17
  94.9 6.9 %all-to-all-done = bf16[2,64,128]{2,0,1:T(2,128)(2,1)S(1)} async-done(((bf16[2,64,128]{2,0,1:T(2,128)(2,1)}), bf16[2,64,128]{2,0,1:T(2,128)(2,1)S(1)}, u32[]{:S(2)}, u32[]{:S(2)}) %all-to-all-start) | async-done | bytes 32800 | tf_op jit(solution)/shard_map/all_to_all | solution.py:55
  102.6 1.3 fusion.16
  105.2 180.9 %all-reduce.8.cloned.1.call-done = f32[128,1792]{1,0:T(8,128)} async-done(((f32[128,1792]{1,0:T(8,128)}), f32[128,1792]{1,0:T(8,128)}) %all-reduce.8.cloned.1.call-update) | async-done | bytes 917520
  286.1 1.0 multiply_reduce_fusion
  287.0 8.6 %psum.14 = f32[2]{0:T(128)S(1)} all-reduce(f32[2]{0:T(128)S(1)} %multiply_reduce_fusion), channel_id=1, replica_groups=mesh['wide'=64,'narrow'=4] {'narrow'}, use_global_device_ids=true, to_apply=%region_5.6 | all-reduce | flops 2 | bytes 16 | tf_op jit(solution)/shard_map/psum | solution.py:66
  295.6 0.9 fusion.23
  296.5 48.1 %all-gather = bf16[64,2,1792]{2,1,0:T(2,128)(2,1)S(1)} all-gather(bf16[1,2,1792]{2,1,0:T(2,128)(2,1)S(1)} %fusion.23), channel_id=1, replica_groups=mesh['wide'=64,'narrow'=4] {'wide'}, dimensions={0}, use_global_device_ids=true | all-gather | bytes 465920 | tf_op jit(solution)/shard_map/all_gather | solution.py:71
  344.8 1.6 fusion.31
  346.5 1.6 fusion.30
  348.1 0.7 pad_maximum_fusion
  349.0 42.7 %all-reduce.6.cloned.1.call-done = f32[128,576]{0,1:T(8,128)} async-done(((f32[128,576]{0,1:T(8,128)}), f32[128,576]{0,1:T(8,128)}) %all-reduce.6.cloned.1.call-update) | async-done | bytes 294928 | tf_op jit(solution)/shard_map/psum | solution.py:79
  391.7 2.8 fusion.9
  394.5 189.7 %all-reduce.10.cloned.1.call-done = f32[128,1792]{1,0:T(8,128)} async-done(((f32[128,1792]{1,0:T(8,128)}), f32[128,1792]{1,0:T(8,128)}) %all-reduce.10.cloned.1.call-update) | async-done | bytes 917520
  584.2 1.5 fusion.20
  (36 shorter events, 3.0 us)
Async XLA Ops:
  6.5 56.8 %copy-start = (bf16[16,128,512]{2,1,0:T(8,128)(2,1)S(1)}, bf16[16,128,512]{2,1,0:T(8,128)(2,1)}, u32[]{:S(2)}) copy-start(bf16[16,128,512]{2,1,0:T(8,128)(2,1)} %param.16) | copy-start | bytes 6291460
  70.8 21.6 %copy-start.4 = (s32[128]{0:T(128)S(1)}, s32[128]{0:T(128)}, u32[]{:S(2)}) copy-start(s32[128]{0:T(128)} %param.20) | copy-start | bytes 1540
  70.8 31.8 %copy-start.1 = (bf16[128,1792]{1,0:T(8,128)(2,1)S(1)}, bf16[128,1792]{1,0:T(8,128)(2,1)}, u32[]{:S(2)}) copy-start(bf16[128,1792]{1,0:T(8,128)(2,1)} %param.21) | copy-start | bytes 1376260
  70.8 33.2 %copy-start.5 = (u32[256]{0:T(256)S(1)}, u32[256]{0:T(256)}, u32[]{:S(2)}) copy-start(u32[256]{0:T(256)} %constant.62) | copy-start | bytes 3076
  70.8 215.3 %copy-start.2 = (bf16[2,1792]{1,0:T(2,128)(2,1)S(1)}, bf16[2,1792]{1,0:T(2,128)(2,1)}, u32[]{:S(2)}) copy-start(bf16[2,1792]{1,0:T(2,128)(2,1)} %param.13) | copy-start | bytes 21508
  70.8 216.2 %copy-start.3 = (bf16[1792]{0:T(1024)(128)(2,1)S(1)}, bf16[1792]{0:T(1024)(128)(2,1)}, u32[]{:S(2)}) copy-start(bf16[1792]{0:T(1024)(128)(2,1)} %param.22) | copy-start | bytes 10756
  85.6 16.3 %all-to-all-start = ((bf16[2,64,128]{2,0,1:T(2,128)(2,1)}), bf16[2,64,128]{2,0,1:T(2,128)(2,1)S(1)}, u32[]{:S(2)}, u32[]{:S(2)}) async-start(bf16[2,64,128]{2,0,1:T(2,128)(2,1)} %all_gather.10), calls=%async_computation | async-start | bytes 65536 | tf_op jit(solution)/shard_map/all_to_all | solution.py:55
  92.3 193.7 %all-reduce.8.cloned.1.call-start = ((), (), s32[]{:S(2)}) async-start(), calls=%async_computation.2 | async-start | bytes 1835008
  103.9 287.8 %all-reduce.6.cloned.1.call-start = ((), (), s32[]{:S(2)}) async-start(), calls=%async_computation.1 | async-start | bytes 589824 | tf_op jit(solution)/shard_map/psum | solution.py:79
  348.9 235.3 %all-reduce.10.cloned.1.call-start = ((), (), s32[]{:S(2)}) async-start(), calls=%async_computation.3 | async-start | bytes 1835008
Sparse Core Ops, SparseCore 0:
  104.0 182.0 all-reduce.7
  349.0 42.5 all-reduce.5
  395.1 189.0 all-reduce.9
where the time goes:
time: 593 us; the launch traced here: 592 us
  waiting for transfers between devices  420 us (71%)
  blocking collectives  123 us (21%)
  matrix products  16.6 us (3%)
  between operations  13.9 us (2%)
  other arithmetic  9.27 us (2%)
  starting transfers between devices  6.87 us (1%)
    unnamed x5, waiting for transfers between devices  371 us
    all_gather x1, blocking collectives, shards(): gathered = lax.all_gather(packed_queries, 'wide', axis=0, tiled=True)  53.8 us
    all_gather x1, blocking collectives, shards(): row_piece = lax.all_gather(normed, 'wide', axis=0, tiled=True)  48.1 us
    psum x1, waiting for transfers between devices, shards(): summed = lax.psum(local_terms, 'narrow')  42.7 us
    all_gather x1, blocking collectives, shards(): every_head = lax.all_gather(heads_out, 'narrow', axis=1, tiled=True)  12.7 us
  transfers between devices with their start and end apart: 4, of which 4 were waited for; matrix products, arithmetic and copies ran while one was open for 1% of the time, Pallas kernels for 0%

commit v1 on v0

--- a/solution.py
+++ b/solution.py
@@ -22,6 +22,23 @@
     up_weight,
     down_weight,
 ):
+
+    def switch_signs(inputs):
+        axis_tag = "narrow"
+        wide_n = lax.psum(1, axis_name=axis_tag)
+
+        def rest_state(y1, v1):
+            if v1 >= wide_n:
+                return y1
+            finding = lax.ppermute(
+                y1, axis_name=axis_tag, perm=list(map(lambda w: (w, w ^ v1), range(wide_n)))
+            )
+            kept_arr = rest_state(y1 + finding, 2 * v1)
+            return kept_arr
+
+        w_next = rest_state(inputs, 1)
+        return w_next
+
     slot_count = latent_cache.shape[0]
     head_size = query_nope.shape[2]
     latent_width = absorb_key.shape[2]
@@ -76,7 +93,7 @@
         ],
         axis=1,
     )
-    summed = lax.psum(local_terms, "narrow")
+    summed = switch_signs(local_terms)
     hidden = (jax.nn.silu(summed[:, :hidden_cols]) * summed[:, hidden_cols:]).astype(jnp.bfloat16)
     ffn_total = lax.psum_scatter(
         jnp.dot(hidden, down_weight, preferred_element_type=jnp.float32),

time: 593 us -> 562 us (0.948)
  waiting for transfers between devices: 420 us -> 389 us
    psum x1 -> x0, waiting for transfers between devices: 42.7 us -> none  [shards(): summed = lax.psum(local_terms, 'narrow')]
    ppermute x0 -> x2, waiting for transfers between devices: none -> 17.4 us  [rest_state(): lax.ppermute(y1, axis_name=axis_tag, perm=list(map(lambda w: (w, w ^ v1),...]
    unnamed x5 -> x4, waiting for transfers between devices: 371 us -> 364 us
  transfers between devices with their start and end apart: 4 -> 5, of which waited for: 4 -> 5; matrix products, arithmetic and copies ran while one was open for 1% -> 1% of each run, Pallas kernels for 0% -> 0%
where the time goes in v1:
time: 562 us
  waiting for transfers between devices  389 us (69%)
  blocking collectives  123 us (22%)
  matrix products  15.3 us (3%)
  between operations  14.2 us (3%)
  starting transfers between devices  9.71 us (2%)
  other arithmetic  8.6 us (2%)
    unnamed x4, waiting for transfers between devices  364 us
    all_gather x1, blocking collectives, shards(): gathered = lax.all_gather(packed_queries, 'wide', axis=0, tiled=True)  53.8 us
    all_gather x1, blocking collectives, shards(): row_piece = lax.all_gather(normed, 'wide', axis=0, tiled=True)  48.1 us
    ppermute x2, waiting for transfers between devices, rest_state(): lax.ppermute(y1, axis_name=axis_tag, perm=list(map(lambda w: (w, w ^ v1),...  17.4 us
    all_gather x1, blocking collectives, shards(): every_head = lax.all_gather(heads_out, 'narrow', axis=1, tiled=True)  12.7 us
  transfers between devices with their start and end apart: 5, of which 5 were waited for; matrix products, arithmetic and copies ran while one was open for 1% of the time, Pallas kernels for 0%

profile of v1, /device:TPU:2, one launch (start us, length us, event | category | flops | bytes accessed | tf_op | source)
XLA Modules:
  0.0 561.8 jit_solution(1390198431209638278)
XLA Ops:
  6.5 0.9 compare_and_fusion
  8.2 53.8 %all_gather.9 = bf16[128,16,192]{2,1,0:T(8,128)(2,1)S(1)} all-gather(bf16[2,16,192]{2,1,0:T(8,128)(2,1)S(1)} %pad_maximum_fusion.1), channel_id=1, replica_groups=mesh['wide'=64,'narrow'=4] {'wide'}, dimensions={0}, use_global_device_ids=true | all-gather | bytes 798720 | tf_op jit(solution)/shard_map/all_gather | solution.py:47
  62.6 0.7 iota_compare_fusion
  63.7 3.1 fusion.4
  67.0 3.7 fusion.7
  70.8 2.0 fusion.5
  72.8 12.7 %all_gather.10 = bf16[2,64,128]{2,0,1:T(2,128)(2,1)} all-gather(bf16[2,16,128]{2,0,1:T(2,128)(2,1)S(1)} %fusion.5), channel_id=1, replica_groups=mesh['wide'=64,'narrow'=4] {'narrow'}, dimensions={1}, use_global_device_ids=true | all-gather | bytes 40960 | tf_op jit(solution)/shard_map/all_gather | solution.py:70
  85.6 6.7 %all-to-all-start = ((bf16[2,64,128]{2,0,1:T(2,128)(2,1)}), bf16[2,64,128]{2,0,1:T(2,128)(2,1)S(1)}, u32[]{:S(2)}, u32[]{:S(2)}) async-start(bf16[2,64,128]{2,0,1:T(2,128)(2,1)} %all_gather.10), calls=%async_computation | async-start | bytes 65536 | tf_op jit(solution)/shard_map/all_to_all | solution.py:72
  92.4 2.5 sort.17
  94.9 6.9 %all-to-all-done = bf16[2,64,128]{2,0,1:T(2,128)(2,1)S(1)} async-done(((bf16[2,64,128]{2,0,1:T(2,128)(2,1)}), bf16[2,64,128]{2,0,1:T(2,128)(2,1)S(1)}, u32[]{:S(2)}, u32[]{:S(2)}) %all-to-all-start) | async-done | bytes 32800 | tf_op jit(solution)/shard_map/all_to_all | solution.py:72
  102.6 1.3 fusion.16
  105.2 180.9 %all-reduce.5.cloned.1.call-done = f32[128,1792]{1,0:T(8,128)} async-done(((f32[128,1792]{1,0:T(8,128)}), f32[128,1792]{1,0:T(8,128)}) %all-reduce.5.cloned.1.call-update) | async-done | bytes 917520
  286.1 1.0 multiply_reduce_fusion
  287.0 8.6 %psum.7 = f32[2]{0:T(128)S(1)} all-reduce(f32[2]{0:T(128)S(1)} %multiply_reduce_fusion), channel_id=1, replica_groups=mesh['wide'=64,'narrow'=4] {'narrow'}, use_global_device_ids=true, to_apply=%region_5.6 | all-reduce | flops 2 | bytes 16 | tf_op jit(solution)/shard_map/psum | solution.py:83
  295.6 0.9 fusion.23
  296.5 48.1 %all-gather = bf16[64,2,1792]{2,1,0:T(2,128)(2,1)S(1)} all-gather(bf16[1,2,1792]{2,1,0:T(2,128)(2,1)S(1)} %fusion.23), channel_id=1, replica_groups=mesh['wide'=64,'narrow'=4] {'wide'}, dimensions={0}, use_global_device_ids=true | all-gather | bytes 465920 | tf_op jit(solution)/shard_map/all_gather | solution.py:88
  344.8 1.6 fusion.32
  346.5 1.7 fusion.31
  348.3 2.5 collective-permute-start
  350.7 7.5 %collective-permute-done = f32[128,576]{0,1:T(8,128)S(1)} collective-permute-done((f32[128,576]{0,1:T(8,128)S(1)}, f32[128,576]{0,1:T(8,128)S(1)}, u32[]{:S(2)}, u32[]{:S(2)}) %collective-permute-start) | collective-permute-done | bytes 294944 | tf_op jit(solution)/shard_map/ppermute | solution.py:33
  358.7 9.9 %collective-permute-done.1 = f32[128,576]{0,1:T(8,128)S(1)} collective-permute-done((f32[128,576]{0,1:T(8,128)S(1)}, f32[128,576]{0,1:T(8,128)S(1)}, u32[]{:S(2)}, u32[]{:S(2)}) %collective-permute-start.1) | collective-permute-done | bytes 294944 | tf_op jit(solution)/shard_map/ppermute | solution.py:33
  368.6 1.4 fusion.9
  370.0 183.5 %all-reduce.7.cloned.1.call-done = f32[128,1792]{1,0:T(8,128)} async-done(((f32[128,1792]{1,0:T(8,128)}), f32[128,1792]{1,0:T(8,128)}) %all-reduce.7.cloned.1.call-update) | async-done | bytes 917520
  553.5 1.5 fusion.20
  (41 shorter events, 4.1 us)
Async XLA Ops:
  6.5 56.8 %copy-start = (bf16[16,128,512]{2,1,0:T(8,128)(2,1)S(1)}, bf16[16,128,512]{2,1,0:T(8,128)(2,1)}, u32[]{:S(2)}) copy-start(bf16[16,128,512]{2,1,0:T(8,128)(2,1)} %param.16) | copy-start | bytes 6291460
  70.8 21.6 %copy-start.5 = (s32[128]{0:T(128)S(1)}, s32[128]{0:T(128)}, u32[]{:S(2)}) copy-start(s32[128]{0:T(128)} %param.20) | copy-start | bytes 1540
  70.8 31.8 %copy-start.2 = (bf16[128,1792]{1,0:T(8,128)(2,1)S(1)}, bf16[128,1792]{1,0:T(8,128)(2,1)}, u32[]{:S(2)}) copy-start(bf16[128,1792]{1,0:T(8,128)(2,1)} %param.21) | copy-start | bytes 1376260
  70.8 33.2 %copy-start.6 = (u32[256]{0:T(256)S(1)}, u32[256]{0:T(256)}, u32[]{:S(2)}) copy-start(u32[256]{0:T(256)} %constant.62) | copy-start | bytes 3076
  70.8 215.3 %copy-start.3 = (bf16[2,1792]{1,0:T(2,128)(2,1)S(1)}, bf16[2,1792]{1,0:T(2,128)(2,1)}, u32[]{:S(2)}) copy-start(bf16[2,1792]{1,0:T(2,128)(2,1)} %param.13) | copy-start | bytes 21508
  70.8 216.2 %copy-start.4 = (bf16[1792]{0:T(1024)(128)(2,1)S(1)}, bf16[1792]{0:T(1024)(128)(2,1)}, u32[]{:S(2)}) copy-start(bf16[1792]{0:T(1024)(128)(2,1)} %param.22) | copy-start | bytes 10756
  85.6 16.3 %all-to-all-start = ((bf16[2,64,128]{2,0,1:T(2,128)(2,1)}), bf16[2,64,128]{2,0,1:T(2,128)(2,1)S(1)}, u32[]{:S(2)}, u32[]{:S(2)}) async-start(bf16[2,64,128]{2,0,1:T(2,128)(2,1)} %all_gather.10), calls=%async_computation | async-start | bytes 65536 | tf_op jit(solution)/shard_map/all_to_all | solution.py:72
  92.3 193.7 %all-reduce.5.cloned.1.call-start = ((), (), s32[]{:S(2)}) async-start(), calls=%async_computation.1 | async-start | bytes 1835008
  103.9 449.6 %all-reduce.7.cloned.1.call-start = ((), (), s32[]{:S(2)}) async-start(), calls=%async_computation.2 | async-start | bytes 1835008
  346.5 22.1 %copy-start.1 = (bf16[288,1792]{1,0:T(8,128)(2,1)S(1)}, bf16[288,1792]{1,0:T(8,128)(2,1)}, u32[]{:S(2)}) copy-start(bf16[288,1792]{1,0:T(8,128)(2,1)} %param.25) | copy-start | bytes 3096580
  348.3 10.0 %collective-permute-start = (f32[128,576]{0,1:T(8,128)S(1)}, f32[128,576]{0,1:T(8,128)S(1)}, u32[]{:S(2)}, u32[]{:S(2)}) collective-permute-start(f32[128,576]{0,1:T(8,128)S(1)} %pad_maximum_fusion), channel_id=1, source_target_pairs={{0,1},{1,0},{2,3},{3,2},{4,5},{5,4},{6,7},{7,6},{8,9},{9,8},{10,11... | collective-permute-start | bytes 884744 | tf_op jit(solution)/shard_map/ppermute | solution.py:33
  358.3 10.3 %collective-permute-start.1 = (f32[128,576]{0,1:T(8,128)S(1)}, f32[128,576]{0,1:T(8,128)S(1)}, u32[]{:S(2)}, u32[]{:S(2)}) collective-permute-start(f32[128,576]{0,1:T(8,128)S(1)} %fusion.29), channel_id=1, source_target_pairs={{0,2},{1,3},{2,0},{3,1},{4,6},{5,7},{6,4},{7,5},{8,10},{9,11},{10,... | collective-permute-start | bytes 884744 | tf_op jit(solution)/shard_map/ppermute | solution.py:33
Sparse Core Ops, SparseCore 0:
  104.0 182.0 all-reduce.4
  370.2 183.3 all-reduce.6
